TPU v7x, 128 devices: a whole 4x4x4 slice. The times are simulated.
128 devices in a mesh: tensor: 8 (over z, core), fsdp: 16 (over x, y).
Axes of the slice: x: 4, y: 4, z: 4, core: 2. Of those that a mesh axis runs over, the one named last changes fastest.
Arguments:
- momentum: float32 [4096, 28672], P('tensor', 'fsdp'), may hold values from -6 to 6
- gradient: bfloat16 [4096, 28672], P('tensor', 'fsdp'), may hold values from -6 to 6
- right_factor: float32 [28672, 512], P('fsdp'), may hold values from -0.03125 to 0.03125
Outputs:
- new_momentum: float32 [4096, 28672], P('tensor', 'fsdp')
- update: float32 [4096, 28672], P('tensor', 'fsdp')
- new_right: float32 [28672, 512], P('fsdp')
All inputs are finite; a program needn't handle non-finite values.
Results may differ from a plain program's by a relative error of at most 0.0003.
Values sent between devices are 32-bit elements; how exact they have to be, the bound alone decides.
A program may use at most 128 MiB of HBM per device.

v0:
```python
import functools
import jax
import jax.numpy as jnp
from jax import lax
from jax.sharding import Mesh
from jax.sharding import PartitionSpec as P

ROWS = 4096
COLS = 28672
RANK = 512
FSDP = ("fsdp_0", "fsdp_1")
TENSOR = ("tensor_0", "tensor_1")
TENSOR_FSDP = ("tensor_0", "tensor_1", "fsdp_0", "fsdp_1")


def total_of_pieces(value, axis):
    parts = lax.all_gather(value, axis)
    return parts.sum(axis=0)


def in_blocks(value, dim, devices):
    lengths = value.shape
    parts = value.reshape(*lengths[:dim], devices, lengths[dim] // devices, *lengths[dim + 1 :])
    return jnp.moveaxis(parts, dim, 0)


def sum_at_owner(value, axis, dim):
    devices = lax.axis_size(axis)
    parts = lax.all_to_all(in_blocks(value, dim, devices), axis, 0, 0, tiled=True)
    return jnp.sum(parts, axis=0)


def over_axes(value, axes):
    return functools.reduce(lax.psum, axes, value)


def inner_rows(first, second):
    return lax.dot_general(
        first,
        second,
        (((0,), (0,)), ((), ())),
        precision=lax.Precision.HIGHEST,
        preferred_element_type=jnp.float32,
    )


def outer_rank(first, second):
    return lax.dot_general(
        first,
        second,
        (((1,), (1,)), ((), ())),
        precision=lax.Precision.HIGHEST,
        preferred_element_type=jnp.float32,
    )


def orthonormal(block, gram):
    lower = jnp.linalg.cholesky(gram)
    return jax.scipy.linalg.solve_triangular(lower, block.T, lower=True).T


def per_device(momentum, gradient, right_factor):
    buffer = momentum + gradient.astype(jnp.float32)
    partial_value = jnp.dot(
        buffer, right_factor, precision=lax.Precision.HIGHEST, preferred_element_type=jnp.float32
    )
    left = lax.psum(partial_value, FSDP)
    gram = total_of_pieces(inner_rows(left, left), TENSOR)
    ortho = orthonormal(left, gram)
    right_part = inner_rows(buffer, ortho)
    right_block = sum_at_owner(right_part, TENSOR, 0)
    colsq = over_axes(jnp.sum(right_block * right_block, axis=0), TENSOR_FSDP)
    right = lax.all_gather(right_block, TENSOR, axis=0, tiled=True)
    normed = right / jnp.sqrt(colsq + 1e-06)
    new_momentum = buffer - 0.05 * outer_rank(ortho, right)
    scale = jnp.sqrt(jnp.float32(ROWS * COLS / RANK))
    update = scale * outer_rank(ortho, normed)
    return (new_momentum, update, normed)


def solution(mesh):
    finer = Mesh(mesh.devices.reshape(4, 2, 4, 4), ("tensor_0", "tensor_1", "fsdp_0", "fsdp_1"))
    placed = (P(TENSOR, FSDP), P(TENSOR, FSDP), P(FSDP, None))
    return jax.shard_map(
        per_device,
        mesh=finer,
        in_specs=placed,
        out_specs=(P(TENSOR, FSDP), P(TENSOR, FSDP), P(FSDP, None)),
        check_vma=False,
    )
```

profile of v0, /device:TPU:0, one launch (start us, length us, event | category | flops | bytes accessed | tf_op | source)
XLA Modules:
  0.0 453.6 jit_solution(2981976357336586488)
XLA Ops:
  7.2 0.0 all-reduce.3.cloned.1.call-start
  7.2 10.3 %fusion.1 = f32[512,512]{1,0:T(8,128)} fusion(f32[1792,512]{1,0:T(8,128)} %param.5, f32[512,1792]{1,0:T(8,128)} %param.3, bf16[512,1792]{1,0:T(8,128)(2,1)} %param.4), kind=kOutput, calls=%fused_computation.7 | convolution fusion | flops 5638979584 | bytes 10223616 | tf_op jit(solution)/shard_map/dot_general | solution.py:64
  17.6 0.0 all-reduce.3.cloned.1.call-update
  17.6 0.0 all-gather.6.cloned.1.call-start
  17.6 89.8 %all-reduce.3.cloned.1.call-done = f32[512,512]{1,0:T(8,128)} async-done(((f32[512,512]{1,0:T(8,128)}), f32[512,512]{1,0:T(8,128)}) %all-reduce.3.cloned.1.call-update) | async-done | bytes 1048592 | tf_op jit(solution)/shard_map/psum | solution.py:67
  107.4 4.5 %fusion.36 = f32[512,512]{1,0:T(8,128)} fusion(f32[512,512]{1,0:T(8,128)} %all-reduce.3.cloned.1.call-done), kind=kOutput, calls=%fused_computation.78 | convolution fusion | flops 1610612736 | bytes 2097152 | tf_op jit(solution)/shard_map/dot_general | solution.py:38
  112.0 0.5 all-gather.4.cloned.1.call-start
  112.5 48.7 %all-gather.6.cloned.1.call-done = f32[4096,512]{1,0:T(8,128)} async-done(((f32[512,512]{1,0:T(8,128)}), f32[4096,512]{1,0:T(8,128)}) %all-gather.6.cloned.1.call-update) | async-done | bytes 8388624 | tf_op jit(solution)/shard_map/all_gather | solution.py:17
  161.2 4.5 reduce_sum.27
  165.7 0.3 copy.7
  166.1 0.2 fusion.2
  166.3 1.0 copy-done.8
  167.3 11.7 %cholesky.104 = f32[128,128]{1,0:T(8,128)S(1)} custom-call(f32[128,128]{1,0:T(8,128)S(1)} %cholesky.266), custom_call_target="Cholesky" | custom-call | tf_op jit(solution)/shard_map/jit(cholesky)/cholesky | solution.py:58
  179.0 0.1 cholesky.224
  179.1 9.8 %custom-call.31 = f32[1,128,128]{1,2,0:T(8,128)S(1)} custom-call(f32[1,128,128]{2,1,0:T(8,128)S(1)} %get-tuple-element.30), custom_call_target="InvertDiagBlocksLowerTriangular" | custom-call | tf_op jit(solution)/shard_map/jit(cholesky)/cholesky | solution.py:58
  189.0 1.2 constant_dynamic-update-slice_fusion.3
  190.2 1.3 convolution_subtract_fusion.3
  191.5 11.9 %cholesky.217 = f32[128,128]{1,0:T(8,128)S(1)} custom-call(f32[128,128]{1,0:T(8,128)S(1)} %cholesky.270), custom_call_target="Cholesky" | custom-call | tf_op jit(solution)/shard_map/jit(cholesky)/cholesky | solution.py:58
  203.4 9.8 %custom-call.32 = f32[1,128,128]{1,2,0:T(8,128)S(1)} custom-call(f32[1,128,128]{2,1,0:T(8,128)S(1)} %get-tuple-element.27), custom_call_target="InvertDiagBlocksLowerTriangular" | custom-call | tf_op jit(solution)/shard_map/jit(cholesky)/cholesky | solution.py:58
  213.2 0.3 convolution_dynamic-update-slice_fusion
  213.5 1.3 convolution_subtract_fusion.4
  214.8 11.7 %cholesky.238 = f32[128,128]{1,0:T(8,128)S(1)} custom-call(f32[128,128]{1,0:T(8,128)S(1)} %cholesky.275), custom_call_target="Cholesky" | custom-call | tf_op jit(solution)/shard_map/jit(cholesky)/cholesky | solution.py:58
  226.5 0.7 compare_reduce_fusion.1
  227.3 9.8 %custom-call.33 = f32[1,128,128]{1,2,0:T(8,128)S(1)} custom-call(f32[1,128,128]{2,1,0:T(8,128)S(1)} %get-tuple-element.24), custom_call_target="InvertDiagBlocksLowerTriangular" | custom-call | tf_op jit(solution)/shard_map/jit(cholesky)/cholesky | solution.py:58
  237.1 0.2 convolution_dynamic-update-slice_fusion.1
  237.3 1.2 convolution_subtract_fusion.5
  238.5 12.1 %cholesky.255 = f32[128,128]{1,0:T(8,128)S(1)} custom-call(f32[128,128]{1,0:T(8,128)S(1)} %convolution_subtract_fusion.5), custom_call_target="Cholesky" | custom-call | tf_op jit(solution)/shard_map/jit(cholesky)/cholesky | solution.py:58
  250.7 0.6 compare_reduce_fusion
  251.3 0.7 compare_reduce_fusion.2
  254.5 1.1 select_select_fusion
  255.6 14.2 %while.1 = (s32[]{:T(128)}, f32[512,512]{1,0:T(8,128)}, s32[4,2]{0,1:T(2,128)S(1)}, f32[4,128,128]{2,1,0:T(8,128)}, s32[]{:T(128)}) while((s32[]{:T(128)}, f32[512,512]{1,0:T(8,128)}, s32[4,2]{0,1:T(2,128)S(1)}, f32[4,128,128]{2,1,0:T(8,128)}, s32[]{:T(128)}) %tuple.31), condition=%wide.while_cond, body=%wide.while_body.sunk | while | flops 2 | bytes 132205 | solution.py:59
  255.6 0.1 constant_dynamic-slice_fusion.2
  255.7 0.6 fusion.48
  256.3 2.9 bitcast_dynamic-update-slice_fusion.2
  259.2 0.1 constant_dynamic-slice_fusion.2
  259.2 0.6 fusion.48
  259.8 2.9 bitcast_dynamic-update-slice_fusion.2
  262.7 0.1 constant_dynamic-slice_fusion.2
  262.8 0.6 fusion.48
  263.4 2.9 bitcast_dynamic-update-slice_fusion.2
  266.3 0.1 constant_dynamic-slice_fusion.2
  266.3 0.6 fusion.48
  266.9 2.8 bitcast_dynamic-update-slice_fusion.2
  269.8 40.1 %custom-call.34 = f32[4,128,128]{1,2,0:T(8,128)S(1)} custom-call(f32[4,128,128]{2,1,0:T(8,128)} %get-tuple-element.10), custom_call_target="InvertDiagBlocksLowerTriangular" | custom-call | tf_op jit(solution)/shard_map/jit(_solve_triangular)/triangular_solve | solution.py:59
  309.9 0.4 fusion.11
  310.4 0.2 copy-done.9
  310.6 1.9 convolution_subtract_fusion.1
  312.5 1.3 fusion.24
  313.7 1.9 convolution_subtract_fusion
  315.6 1.3 fusion.22
  316.9 2.5 convolution_subtract_fusion.2
  319.4 1.3 fusion.21
  320.7 12.3 %fusion = f32[1792,512]{1,0:T(8,128)S(1)} fusion(f32[512,1792]{1,0:T(8,128)S(1)} %copy-done, bf16[512,1792]{1,0:T(8,128)(2,1)S(1)} %copy-done.2, f32[128,512]{1,0:T(8,128)S(1)} %fusion.21, f32[128,512]{1,0:T(8,128)S(1)} %fusion.22, f32[128,512]{1,0:T(8,128)S(1)} %fusion.24, f32[128,512]{1,0:T(8,128)S(1)} %fusion.11), kind=kOutput, calls=%fused_computation.6 | convolution fusion | flops 5639766016 | bytes 10223616 | tf_op jit(solution)/shard_map/dot_general | solution.py:38
  333.0 47.3 %all_to_all.5 = f32[8,224,512]{2,1,0:T(8,128)} all-to-all(f32[8,224,512]{2,1,0:T(8,128)S(1)} %bitcast.56), channel_id=1, replica_groups=mesh['tensor_0'=4,'tensor_1'=2,'fsdp_0'=4,'fsdp_1'=4] {'tensor_0','tenso..., dimensions={0} | all-to-all | bytes 7340032 | tf_op jit(solution)/shard_map/all_to_all | solution.py:29
  380.3 3.3 reduce_sum.28
  383.6 1.1 multiply_reduce_fusion
  384.6 8.9 %psum.36 = f32[512]{0:T(512)S(1)} all-reduce(f32[512]{0:T(512)S(1)} %multiply_reduce_fusion), channel_id=1, replica_groups=mesh['tensor_0'=4,'tensor_1'=2,'fsdp_0'=4,'fsdp_1'=4] {'tensor_0'}, use_global_device_ids=true, to_apply=%region_12.13 | all-reduce | flops 512 | bytes 4096 | tf_op jit(solution)/shard_map/psum | solution.py:34
  393.5 2.5 psum.37
  396.0 10.4 %psum.38 = f32[512]{0:T(512)S(1)} all-reduce(f32[512]{0:T(512)S(1)} %psum.37), channel_id=1, replica_groups=mesh['tensor_0'=4,'tensor_1'=2,'fsdp_0'=4,'fsdp_1'=4] {'fsdp_0'}, use_global_device_ids=true, to_apply=%region_14.15 | all-reduce | flops 512 | bytes 4096 | tf_op jit(solution)/shard_map/psum | solution.py:34
  406.4 10.5 %psum.39 = f32[512]{0:T(512)S(1)} all-reduce(f32[512]{0:T(512)S(1)} %psum.38), channel_id=1, replica_groups=mesh['tensor_0'=4,'tensor_1'=2,'fsdp_0'=4,'fsdp_1'=4] {'fsdp_1'}, use_global_device_ids=true, to_apply=%region_15.16 | all-reduce | flops 512 | bytes 4096 | tf_op jit(solution)/shard_map/psum | solution.py:34
  416.8 0.0 all-gather.4.cloned.1.call-done
  416.9 2.5 broadcast_divide_fusion
  419.5 13.7 %convolution_multiply_fusion = f32[512,1792]{1,0:T(8,128)} fusion(f32[1792,512]{1,0:T(8,128)S(1)} %broadcast_divide_fusion, f32[128,512]{1,0:T(8,128)S(1)} %fusion.21, f32[128,512]{1,0:T(8,128)S(1)} %copy-done.7, f32[128,512]{1,0:T(8,128)S(1)} %fusion.24, f32[128,512]{1,0:T(8,128)S(1)} %fusion.11), kind=kOutput, calls=%fused_computation.4 | convolution fusion | flops 5638848512 | bytes 8388608 | tf_op jit(solution)/shard_map/dot_general | solution.py:48
  433.2 13.7 %multiply_subtract_fusion = f32[512,1792]{1,0:T(8,128)} fusion(f32[1792,512]{1,0:T(8,128)S(1)} %copy-done.4, f32[512,1792]{1,0:T(8,128)S(1)} %copy-done.1, bf16[512,1792]{1,0:T(8,128)(2,1)S(1)} %copy-done.2, f32[128,512]{1,0:T(8,128)S(1)} %fusion.21, f32[128,512]{1,0:T(8,128)S(1)} %copy-done.7, f32[128,512]{1,0:T(8,128)S(1)} %fusion.24, ...), kind=kOutput, calls=%fused_computation.2 | convolution fusion | flops 5641601024 | bytes 13893632 | tf_op jit(solution)/shard_map/dot_general | solution.py:48
  (31 shorter events, 0.3 us)
Async XLA Ops:
  7.2 100.2 %all-reduce.3.cloned.1.call-start = ((), (), s32[]{:S(2)}) async-start(), calls=%async_computation.1 | async-start | bytes 2097152 | tf_op jit(solution)/shard_map/psum | solution.py:67
  17.6 143.6 %all-gather.6.cloned.1.call-start = ((), (), s32[]{:S(2)}) async-start(), calls=%async_computation.3 | async-start | bytes 9437184 | tf_op jit(solution)/shard_map/all_gather | solution.py:17
  112.0 304.9 %all-gather.4.cloned.1.call-start = ((), (), s32[]{:S(2)}) async-start(), calls=%async_computation.2 | async-start | bytes 4128768 | tf_op jit(solution)/shard_map/all_gather | solution.py:73
  166.3 1.0 copy-start.8
  179.0 130.9 %copy-start.5 = (f32[512,512]{1,0:T(8,128)S(1)}, f32[512,512]{1,0:T(8,128)}, u32[]{:S(2)}) copy-start(f32[512,512]{1,0:T(8,128)} %all-reduce.3.cloned.1.call-done) | copy-start | bytes 3145732
  255.6 65.1 %copy-start.2 = (bf16[512,1792]{1,0:T(8,128)(2,1)S(1)}, bf16[512,1792]{1,0:T(8,128)(2,1)}, u32[]{:S(2)}) copy-start(bf16[512,1792]{1,0:T(8,128)(2,1)} %param.4) | copy-start | bytes 5505028
  309.9 0.7 copy-start.9
  309.9 10.8 %copy-start = (f32[512,1792]{1,0:T(8,128)S(1)}, f32[512,1792]{1,0:T(8,128)}, u32[]{:S(2)}) copy-start(f32[512,1792]{1,0:T(8,128)} %param.3) | copy-start | bytes 11010052
  316.9 16.1 %copy-start.6 = (f32[128,512]{1,0:T(8,128)}, f32[128,512]{1,0:T(8,128)S(1)}, u32[]{:S(2)}) copy-start(f32[128,512]{1,0:T(8,128)S(1)} %fusion.22) | copy-start | bytes 786436
  416.8 2.6 copy-start.7
  419.4 13.7 %copy-start.3 = (f32[1792,512]{1,0:T(8,128)}, f32[1792,512]{1,0:T(8,128)S(1)}, u32[]{:S(2)}) copy-start(f32[1792,512]{1,0:T(8,128)S(1)} %broadcast_divide_fusion) | copy-start | bytes 11010052
  419.4 13.7 %copy-start.1 = (f32[512,1792]{1,0:T(8,128)S(1)}, f32[512,1792]{1,0:T(8,128)}, u32[]{:S(2)}) copy-start(f32[512,1792]{1,0:T(8,128)} %param.3) | copy-start | bytes 11010052
  419.4 13.7 %copy-start.4 = (f32[1792,512]{1,0:T(8,128)S(1)}, f32[1792,512]{1,0:T(8,128)}, u32[]{:S(2)}) copy-start(f32[1792,512]{1,0:T(8,128)} %all-gather.4.cloned.1.call-done) | copy-start | bytes 11010052
Sparse Core Ops, SparseCore 0:
  17.7 89.6 all-reduce.2
  112.1 49.0 all-gather.5
  383.7 29.3 all-gather.3
where the time goes:
time: 459 us; the launch traced here: 454 us
  waiting for transfers between devices  139 us (30%)
  other arithmetic  132 us (29%)
  blocking collectives  79.5 us (17%)
  matrix products  70.5 us (15%)
  between operations  16.8 us (4%)
  local copies, waits for them, and re-layouts  15.9 us (3%)
    psum x1, waiting for transfers between devices, per_device(): left = lax.psum(partial_value, FSDP)  89.8 us
    another operation x14, other arithmetic, orthonormal(): lower = jnp.linalg.cholesky(gram)  79 us
    all_gather x1, waiting for transfers between devices, total_of_pieces(): parts = lax.all_gather(value, axis)  48.7 us
    all_to_all x1, blocking collectives, sum_at_owner(): lax.all_to_all(in_blocks(value, dim, devices), axis, 0, 0, tiled=True)  47.3 us
    another operation x3, other arithmetic, orthonormal(): return jax.scipy.linalg.solve_triangular(lower, block.T, lower=True).T  41.2 us
    psum x4, blocking collectives, over_axes(): return functools.reduce(lax.psum, axes, value)  32.2 us
    dot_general x2, matrix products, outer_rank(): lax.dot_general(first, second, (((1,), (1,)), ((), ())), precision=lax.Pr...  27.4 us
    dot_general x2, matrix products, inner_rows(): lax.dot_general(first, second, (((0,), (0,)), ((), ())), precision=lax.Pr...  16.8 us
  transfers between devices with their start and end apart: 3, of which 2 were waited for; matrix products, arithmetic and copies ran while one was open for 0% of the time, Pallas kernels for 0%

commit v1 on v0

--- a/solution.py
+++ b/solution.py
@@ -64,7 +64,7 @@
     partial_value = jnp.dot(
         buffer, right_factor, precision=lax.Precision.HIGHEST, preferred_element_type=jnp.float32
     )
-    left = lax.psum(partial_value, FSDP)
+    left = lax.psum(lax.psum(partial_value, "fsdp_1"), "fsdp_0")
     gram = total_of_pieces(inner_rows(left, left), TENSOR)
     ortho = orthonormal(left, gram)
     right_part = inner_rows(buffer, ortho)

time: 459 us -> 469 us (1.022)
  waiting for transfers between devices: 139 us -> 148 us
    psum x1 -> x2, waiting for transfers between devices: 89.8 us -> 98 us  [per_device(): left = lax.psum(lax.psum(partial_value, 'fsdp_1'), 'fsdp_0')]
  transfers between devices with their start and end apart: 3 -> 4, of which waited for: 2 -> 3; matrix products, arithmetic and copies ran while one was open for 0% -> 0% of each run, Pallas kernels for 0% -> 0%
where the time goes in v1:
time: 469 us; the launch traced here: 464 us
  waiting for transfers between devices  148 us (32%)
  other arithmetic  132 us (28%)
  blocking collectives  79.5 us (17%)
  matrix products  70.5 us (15%)
  between operations  16.8 us (4%)
  local copies, waits for them, and re-layouts  15.9 us (3%)
    psum x2, waiting for transfers between devices, per_device(): left = lax.psum(lax.psum(partial_value, 'fsdp_1'), 'fsdp_0')  98 us
    another operation x14, other arithmetic, orthonormal(): lower = jnp.linalg.cholesky(gram)  79 us
    all_gather x1, waiting for transfers between devices, total_of_pieces(): parts = lax.all_gather(value, axis)  50.4 us
    all_to_all x1, blocking collectives, sum_at_owner(): lax.all_to_all(in_blocks(value, dim, devices), axis, 0, 0, tiled=True)  47.3 us
    another operation x3, other arithmetic, orthonormal(): return jax.scipy.linalg.solve_triangular(lower, block.T, lower=True).T  41.2 us
    psum x4, blocking collectives, over_axes(): return functools.reduce(lax.psum, axes, value)  32.2 us
    dot_general x2, matrix products, outer_rank(): lax.dot_general(first, second, (((1,), (1,)), ((), ())), precision=lax.Pr...  27.4 us
    dot_general x2, matrix products, inner_rows(): lax.dot_general(first, second, (((0,), (0,)), ((), ())), precision=lax.Pr...  16.8 us
  transfers between devices with their start and end apart: 4, of which 3 were waited for; matrix products, arithmetic and copies ran while one was open for 0% of the time, Pallas kernels for 0%

profile of v1, /device:TPU:0, one launch (start us, length us, event | category | flops | bytes accessed | tf_op | source)
XLA Modules:
  0.0 463.6 jit_solution(1891172943867786301)
XLA Ops:
  7.2 0.0 all-reduce.4.cloned.1.call-start
  7.2 10.3 %fusion.1 = f32[512,512]{1,0:T(8,128)} fusion(f32[1792,512]{1,0:T(8,128)} %param.5, f32[512,1792]{1,0:T(8,128)} %param.3, bf16[512,1792]{1,0:T(8,128)(2,1)} %param.4), kind=kOutput, calls=%fused_computation.7 | convolution fusion | flops 5638979584 | bytes 10223616 | tf_op jit(solution)/shard_map/dot_general | solution.py:64
  17.6 0.0 all-reduce.6.cloned.1.call-start
  17.6 48.7 %all-reduce.4.cloned.1.call-done = f32[512,512]{1,0:T(8,128)} async-done(((f32[512,512]{1,0:T(8,128)}), f32[512,512]{1,0:T(8,128)}) %all-reduce.4.cloned.1.call-update) | async-done | bytes 1048592 | tf_op jit(solution)/shard_map/psum | solution.py:67
  66.4 0.0 all-gather.6.cloned.1.call-start
  66.4 49.3 %all-reduce.6.cloned.1.call-done = f32[512,512]{1,0:T(8,128)} async-done(((f32[512,512]{1,0:T(8,128)}), f32[512,512]{1,0:T(8,128)}) %all-reduce.6.cloned.1.call-update) | async-done | bytes 1048592 | tf_op jit(solution)/shard_map/psum | solution.py:67
  115.7 4.5 fusion.36
  120.2 0.5 all-gather.4.cloned.1.call-start
  120.8 50.4 %all-gather.6.cloned.1.call-done = f32[4096,512]{1,0:T(8,128)} async-done(((f32[512,512]{1,0:T(8,128)}), f32[4096,512]{1,0:T(8,128)}) %all-gather.6.cloned.1.call-update) | async-done | bytes 8388624 | tf_op jit(solution)/shard_map/all_gather | solution.py:17
  171.2 4.5 reduce_sum.27
  175.7 0.3 copy.7
  176.0 0.2 fusion.2
  176.3 1.0 copy-done.8
  177.3 11.7 %cholesky.104 = f32[128,128]{1,0:T(8,128)S(1)} custom-call(f32[128,128]{1,0:T(8,128)S(1)} %cholesky.266), custom_call_target="Cholesky" | custom-call | tf_op jit(solution)/shard_map/jit(cholesky)/cholesky | solution.py:58
  189.0 0.1 cholesky.224
  189.1 9.8 %custom-call.31 = f32[1,128,128]{1,2,0:T(8,128)S(1)} custom-call(f32[1,128,128]{2,1,0:T(8,128)S(1)} %get-tuple-element.30), custom_call_target="InvertDiagBlocksLowerTriangular" | custom-call | tf_op jit(solution)/shard_map/jit(cholesky)/cholesky | solution.py:58
  199.0 1.2 constant_dynamic-update-slice_fusion.3
  200.2 1.3 convolution_subtract_fusion.3
  201.5 11.9 %cholesky.217 = f32[128,128]{1,0:T(8,128)S(1)} custom-call(f32[128,128]{1,0:T(8,128)S(1)} %cholesky.270), custom_call_target="Cholesky" | custom-call | tf_op jit(solution)/shard_map/jit(cholesky)/cholesky | solution.py:58
  213.4 9.8 %custom-call.32 = f32[1,128,128]{1,2,0:T(8,128)S(1)} custom-call(f32[1,128,128]{2,1,0:T(8,128)S(1)} %get-tuple-element.27), custom_call_target="InvertDiagBlocksLowerTriangular" | custom-call | tf_op jit(solution)/shard_map/jit(cholesky)/cholesky | solution.py:58
  223.2 0.3 convolution_dynamic-update-slice_fusion
  223.5 1.3 convolution_subtract_fusion.4
  224.8 11.7 %cholesky.238 = f32[128,128]{1,0:T(8,128)S(1)} custom-call(f32[128,128]{1,0:T(8,128)S(1)} %cholesky.275), custom_call_target="Cholesky" | custom-call | tf_op jit(solution)/shard_map/jit(cholesky)/cholesky | solution.py:58
  236.5 0.7 compare_reduce_fusion.1
  237.2 9.8 %custom-call.33 = f32[1,128,128]{1,2,0:T(8,128)S(1)} custom-call(f32[1,128,128]{2,1,0:T(8,128)S(1)} %get-tuple-element.24), custom_call_target="InvertDiagBlocksLowerTriangular" | custom-call | tf_op jit(solution)/shard_map/jit(cholesky)/cholesky | solution.py:58
  247.0 0.2 convolution_dynamic-update-slice_fusion.1
  247.3 1.2 convolution_subtract_fusion.5
  248.5 12.1 %cholesky.255 = f32[128,128]{1,0:T(8,128)S(1)} custom-call(f32[128,128]{1,0:T(8,128)S(1)} %convolution_subtract_fusion.5), custom_call_target="Cholesky" | custom-call | tf_op jit(solution)/shard_map/jit(cholesky)/cholesky | solution.py:58
  260.6 0.6 compare_reduce_fusion
  261.3 0.7 compare_reduce_fusion.2
  264.5 1.1 select_select_fusion
  265.6 14.2 %while.1 = (s32[]{:T(128)}, f32[512,512]{1,0:T(8,128)}, s32[4,2]{0,1:T(2,128)S(1)}, f32[4,128,128]{2,1,0:T(8,128)}, s32[]{:T(128)}) while((s32[]{:T(128)}, f32[512,512]{1,0:T(8,128)}, s32[4,2]{0,1:T(2,128)S(1)}, f32[4,128,128]{2,1,0:T(8,128)}, s32[]{:T(128)}) %tuple.31), condition=%wide.while_cond, body=%wide.while_body.sunk | while | flops 2 | bytes 132205 | solution.py:59
  265.6 0.1 constant_dynamic-slice_fusion.2
  265.6 0.6 fusion.48
  266.3 2.9 bitcast_dynamic-update-slice_fusion.2
  269.1 0.1 constant_dynamic-slice_fusion.2
  269.2 0.6 fusion.48
  269.8 2.9 bitcast_dynamic-update-slice_fusion.2
  272.7 0.1 constant_dynamic-slice_fusion.2
  272.8 0.6 fusion.48
  273.4 2.9 bitcast_dynamic-update-slice_fusion.2
  276.2 0.1 constant_dynamic-slice_fusion.2
  276.3 0.6 fusion.48
  276.9 2.8 bitcast_dynamic-update-slice_fusion.2
  279.7 40.1 %custom-call.34 = f32[4,128,128]{1,2,0:T(8,128)S(1)} custom-call(f32[4,128,128]{2,1,0:T(8,128)} %get-tuple-element.10), custom_call_target="InvertDiagBlocksLowerTriangular" | custom-call | tf_op jit(solution)/shard_map/jit(_solve_triangular)/triangular_solve | solution.py:59
  319.9 0.4 fusion.11
  320.3 0.2 copy-done.9
  320.6 1.9 convolution_subtract_fusion.1
  322.4 1.3 fusion.24
  323.7 1.9 convolution_subtract_fusion
  325.6 1.3 fusion.22
  326.9 2.5 convolution_subtract_fusion.2
  329.4 1.3 fusion.21
  330.7 12.3 %fusion = f32[1792,512]{1,0:T(8,128)S(1)} fusion(f32[512,1792]{1,0:T(8,128)S(1)} %copy-done, bf16[512,1792]{1,0:T(8,128)(2,1)S(1)} %copy-done.2, f32[128,512]{1,0:T(8,128)S(1)} %fusion.21, f32[128,512]{1,0:T(8,128)S(1)} %fusion.22, f32[128,512]{1,0:T(8,128)S(1)} %fusion.24, f32[128,512]{1,0:T(8,128)S(1)} %fusion.11), kind=kOutput, calls=%fused_computation.6 | convolution fusion | flops 5639766016 | bytes 10223616 | tf_op jit(solution)/shard_map/dot_general | solution.py:38
  343.0 47.3 %all_to_all.5 = f32[8,224,512]{2,1,0:T(8,128)} all-to-all(f32[8,224,512]{2,1,0:T(8,128)S(1)} %bitcast.56), channel_id=1, replica_groups=mesh['tensor_0'=4,'tensor_1'=2,'fsdp_0'=4,'fsdp_1'=4] {'tensor_0','tenso..., dimensions={0} | all-to-all | bytes 7340032 | tf_op jit(solution)/shard_map/all_to_all | solution.py:29
  390.3 3.3 reduce_sum.28
  393.5 1.1 multiply_reduce_fusion
  394.6 8.9 %psum.44 = f32[512]{0:T(512)S(1)} all-reduce(f32[512]{0:T(512)S(1)} %multiply_reduce_fusion), channel_id=1, replica_groups=mesh['tensor_0'=4,'tensor_1'=2,'fsdp_0'=4,'fsdp_1'=4] {'tensor_0'}, use_global_device_ids=true, to_apply=%region_13.14 | all-reduce | flops 512 | bytes 4096 | tf_op jit(solution)/shard_map/psum | solution.py:34
  403.5 2.5 psum.45
  406.0 10.4 %psum.46 = f32[512]{0:T(512)S(1)} all-reduce(f32[512]{0:T(512)S(1)} %psum.45), channel_id=1, replica_groups=mesh['tensor_0'=4,'tensor_1'=2,'fsdp_0'=4,'fsdp_1'=4] {'fsdp_0'}, use_global_device_ids=true, to_apply=%region_15.16 | all-reduce | flops 512 | bytes 4096 | tf_op jit(solution)/shard_map/psum | solution.py:34
  416.4 10.5 %psum.47 = f32[512]{0:T(512)S(1)} all-reduce(f32[512]{0:T(512)S(1)} %psum.46), channel_id=1, replica_groups=mesh['tensor_0'=4,'tensor_1'=2,'fsdp_0'=4,'fsdp_1'=4] {'fsdp_1'}, use_global_device_ids=true, to_apply=%region_16.17 | all-reduce | flops 512 | bytes 4096 | tf_op jit(solution)/shard_map/psum | solution.py:34
  426.9 2.5 broadcast_divide_fusion
  429.4 13.7 %convolution_multiply_fusion = f32[512,1792]{1,0:T(8,128)} fusion(f32[1792,512]{1,0:T(8,128)S(1)} %broadcast_divide_fusion, f32[128,512]{1,0:T(8,128)S(1)} %fusion.21, f32[128,512]{1,0:T(8,128)S(1)} %copy-done.7, f32[128,512]{1,0:T(8,128)S(1)} %fusion.24, f32[128,512]{1,0:T(8,128)S(1)} %fusion.11), kind=kOutput, calls=%fused_computation.4 | convolution fusion | flops 5638848512 | bytes 8388608 | tf_op jit(solution)/shard_map/dot_general | solution.py:48
  443.2 13.7 %multiply_subtract_fusion = f32[512,1792]{1,0:T(8,128)} fusion(f32[1792,512]{1,0:T(8,128)S(1)} %copy-done.4, f32[512,1792]{1,0:T(8,128)S(1)} %copy-done.1, bf16[512,1792]{1,0:T(8,128)(2,1)S(1)} %copy-done.2, f32[128,512]{1,0:T(8,128)S(1)} %fusion.21, f32[128,512]{1,0:T(8,128)S(1)} %copy-done.7, f32[128,512]{1,0:T(8,128)S(1)} %fusion.24, ...), kind=kOutput, calls=%fused_computation.2 | convolution fusion | flops 5641601024 | bytes 13893632 | tf_op jit(solution)/shard_map/dot_general | solution.py:48
  (34 shorter events, 0.3 us)
Async XLA Ops:
  7.2 59.2 %all-reduce.4.cloned.1.call-start = ((), (), s32[]{:S(2)}) async-start(), calls=%async_computation.1 | async-start | bytes 2097152 | tf_op jit(solution)/shard_map/psum | solution.py:67
  17.6 98.1 %all-reduce.6.cloned.1.call-start = ((), (), s32[]{:S(2)}) async-start(), calls=%async_computation.2 | async-start | bytes 2097152 | tf_op jit(solution)/shard_map/psum | solution.py:67
  66.4 104.9 %all-gather.6.cloned.1.call-start = ((), (), s32[]{:S(2)}) async-start(), calls=%async_computation.4 | async-start | bytes 9437184 | tf_op jit(solution)/shard_map/all_gather | solution.py:17
  120.2 306.6 %all-gather.4.cloned.1.call-start = ((), (), s32[]{:S(2)}) async-start(), calls=%async_computation.3 | async-start | bytes 4128768 | tf_op jit(solution)/shard_map/all_gather | solution.py:73
  176.3 1.0 copy-start.8
  189.0 130.9 %copy-start.5 = (f32[512,512]{1,0:T(8,128)S(1)}, f32[512,512]{1,0:T(8,128)}, u32[]{:S(2)}) copy-start(f32[512,512]{1,0:T(8,128)} %all-reduce.6.cloned.1.call-done) | copy-start | bytes 3145732
  265.6 65.1 %copy-start.2 = (bf16[512,1792]{1,0:T(8,128)(2,1)S(1)}, bf16[512,1792]{1,0:T(8,128)(2,1)}, u32[]{:S(2)}) copy-start(bf16[512,1792]{1,0:T(8,128)(2,1)} %param.4) | copy-start | bytes 5505028
  319.9 0.7 copy-start.9
  319.9 10.8 %copy-start = (f32[512,1792]{1,0:T(8,128)S(1)}, f32[512,1792]{1,0:T(8,128)}, u32[]{:S(2)}) copy-start(f32[512,1792]{1,0:T(8,128)} %param.3) | copy-start | bytes 11010052
  326.9 16.1 %copy-start.6 = (f32[128,512]{1,0:T(8,128)}, f32[128,512]{1,0:T(8,128)S(1)}, u32[]{:S(2)}) copy-start(f32[128,512]{1,0:T(8,128)S(1)} %fusion.22) | copy-start | bytes 786436
  426.8 2.6 copy-start.7
  429.4 13.7 %copy-start.3 = (f32[1792,512]{1,0:T(8,128)}, f32[1792,512]{1,0:T(8,128)S(1)}, u32[]{:S(2)}) copy-start(f32[1792,512]{1,0:T(8,128)S(1)} %broadcast_divide_fusion) | copy-start | bytes 11010052
  429.4 13.7 %copy-start.1 = (f32[512,1792]{1,0:T(8,128)S(1)}, f32[512,1792]{1,0:T(8,128)}, u32[]{:S(2)}) copy-start(f32[512,1792]{1,0:T(8,128)} %param.3) | copy-start | bytes 11010052
  429.4 13.7 %copy-start.4 = (f32[1792,512]{1,0:T(8,128)S(1)}, f32[1792,512]{1,0:T(8,128)}, u32[]{:S(2)}) copy-start(f32[1792,512]{1,0:T(8,128)} %all-gather.4.cloned.1.call-done) | copy-start | bytes 11010052
Sparse Core Ops, SparseCore 0:
  17.7 48.5 all-reduce.3
  68.7 46.9 all-reduce.5
  120.4 50.8 all-gather.5
  393.7 29.3 all-gather.3
